TPU v7x, 512 devices: a whole 4x4x16 slice. The times are simulated.
512 devices in a mesh: dp: 32 (over z, y_lo), fsdp: 16 (over x, y_hi, core).
Axes of the slice: x: 4, y: 4 (y_hi: 2, y_lo: 2; y = y_hi * 2 + y_lo), z: 16, core: 2. Of those that a mesh axis runs over, the one named last changes fastest.
Arguments:
- tokens: bfloat16 [65536, 1024], P(('dp', 'fsdp')), may hold values from -6 to 6
- cotangent: bfloat16 [65536, 1024], P(('dp', 'fsdp')), may hold values from -6 to 6
- routes: int32 [65536, 1], P(('dp', 'fsdp')), may hold values from 0 to 32; in each aligned block of 128 rows (0 to 127, 128 to 255, ...) at most 4 rows name the same one
- norm_gain_vector: float32 [1024], replicated, may hold values from 0.25 to 1.75
- up_weight: bfloat16 [1024, 4096], P(None, 'fsdp'), may hold values from -0.1875 to 0.1875
- up_bias: float32 [4096], P('fsdp'), may hold values from -4 to 4
- down_weight: bfloat16 [4096, 1024], P('fsdp'), may hold values from -0.09375 to 0.09375
Outputs:
- input_grad: bfloat16 [65536, 1024], P(('dp', 'fsdp'))
- up_grad: float32 [1024, 4096], P(None, 'fsdp')
- bias_grad: float32 [4096], P('fsdp')
- down_grad: float32 [4096, 1024], P('fsdp')
- gain_grad: float32 [1024], replicated
Inputs may be any that keep to these rules, and one draw needn't show every extreme that they name: `routes`: among the 128 slots of one device no value below 32 appears more than 4 times; the value 32 marks a padding slot.
All inputs are finite; a program needn't handle non-finite values.
Results may differ from a plain program's by a relative error of at most 0.024.
Values may be sent and summed in bfloat16 or wider, within the bound.
A program may use at most 128 MiB of HBM per device.

v0:
```python
import jax
import jax.numpy as jnp
from jax import lax
from jax.sharding import Mesh
from jax.sharding import PartitionSpec as P

DP = ("dp_0", "dp_1")
FSDP = ("fsdp_0", "fsdp_1", "fsdp_2")
ROWS_AXES = ("fsdp_0", "fsdp_1")
DP_FSDP = ("dp_0", "dp_1", "fsdp_0", "fsdp_1", "fsdp_2")
root_two_pi = 0.7978845608
cubic = 0.044715


def side_by_side(arrays, axis, split_dim, concat_dim, along):
    both = jnp.concatenate(arrays, axis=along)
    filled, at, finished = (
        lax.all_to_all(both, axis, split_axis=split_dim, concat_axis=concat_dim, tiled=True),
        0,
        [],
    )
    for a in arrays:
        finished.append(lax.slice_in_dim(filled, at, at + a.shape[along], axis=along))
        at += a.shape[along]
    return tuple(finished)


def gelu_pair(pre):
    inner = root_two_pi * (pre + cubic * pre * pre * pre)
    tangent = jnp.tanh(inner)
    act = 0.5 * pre * (1.0 + tangent)
    slope = 0.5 * (1.0 + tangent) + 0.5 * pre * (1.0 - tangent * tangent) * root_two_pi * (
        1.0 + 3.0 * cubic * pre * pre
    )
    return (act, slope)


def apply_layer_norm(values):
    row_average = jnp.mean(values, axis=1, keepdims=True)
    centered = values - row_average
    variance = jnp.mean(centered * centered, axis=1, keepdims=True)
    inverse_std = 1.0 / jnp.sqrt(variance + 1e-05)
    return (centered * inverse_std, inverse_std)


def shards(tokens, cotangent, routes, norm_gain_vector, up_weight, up_bias, down_weight):
    particle_slot_count = tokens.shape[0]
    dp_size = lax.axis_size(DP)
    capacity = particle_slot_count // dp_size
    up_weight = lax.all_gather(up_weight, "fsdp_2", axis=1, tiled=True)
    down_weight = lax.all_gather(down_weight, "fsdp_2", axis=0, tiled=True)
    up_bias = lax.all_gather(up_bias, "fsdp_2", axis=0, tiled=True)
    target = routes[:, 0]
    matches = (target[:, None] == jnp.arange(dp_size + 1, dtype=jnp.int32)[None, :]).astype(
        jnp.int32
    )
    earlier = jnp.cumsum(matches, axis=0) - matches
    ranked = jnp.sum(earlier * matches, axis=1)
    slot_index = jnp.where(target < dp_size, target * capacity + ranked, -1)
    placing = (
        slot_index[None, :] == jnp.arange(particle_slot_count, dtype=jnp.int32)[:, None]
    ).astype(jnp.bfloat16)
    send_in = jnp.dot(placing, tokens, preferred_element_type=jnp.float32).astype(jnp.bfloat16)
    send_cot = jnp.dot(placing, cotangent, preferred_element_type=jnp.float32).astype(jnp.bfloat16)
    packed_in, packed_cot = side_by_side((send_in, send_cot), DP, 0, 0, 1)
    local_standardized, own_inverse = apply_layer_norm(packed_in.astype(jnp.float32))
    normed_local = (local_standardized * norm_gain_vector).astype(jnp.bfloat16)
    all_cot = lax.all_gather(packed_cot, ROWS_AXES, axis=0, tiled=True)
    gathered_normed_rows = lax.all_gather(normed_local, ROWS_AXES, axis=0, tiled=True)
    pre = jnp.dot(gathered_normed_rows, up_weight, preferred_element_type=jnp.float32) + up_bias
    act_full, slope = gelu_pair(pre)
    act = act_full.astype(jnp.bfloat16)
    act_grad = jnp.einsum("rd,kd->rk", all_cot, down_weight, preferred_element_type=jnp.float32)
    pre_grad = (act_grad * slope).astype(jnp.bfloat16)
    down_part = jnp.einsum("rk,rd->kd", act, all_cot, preferred_element_type=jnp.float32)
    up_part = jnp.einsum(
        "rk,rd->kd", pre_grad, gathered_normed_rows, preferred_element_type=jnp.float32
    )
    bias_part = jnp.sum(pre_grad.astype(jnp.float32), axis=0)
    partial_gain_grad = (
        jnp.sum(up_part * up_weight.T.astype(jnp.float32), axis=0) / norm_gain_vector
    )
    parts = jnp.concatenate([up_part, down_part], axis=1).astype(jnp.bfloat16)
    mine = lax.psum_scatter(parts, "fsdp_2", scatter_dimension=0, tiled=True)
    mine = lax.psum_scatter(mine, DP, scatter_dimension=0, tiled=True)
    whole = lax.all_gather(mine, DP, axis=0, tiled=True).astype(jnp.float32)
    d = up_weight.shape[0]
    up_grad = whole[:, :d].T
    down_grad = whole[:, d:]
    normed_rows_gradient = lax.psum_scatter(
        jnp.einsum("rk,dk->rd", pre_grad, up_weight, preferred_element_type=jnp.float32).astype(
            jnp.bfloat16
        ),
        ROWS_AXES,
        scatter_dimension=0,
        tiled=True,
    ).astype(jnp.float32)
    index = lax.axis_index(FSDP)
    k = bias_part.shape[0] // 2
    wide = jnp.zeros((8, 2 * k), jnp.float32)
    wide = lax.dynamic_update_slice(wide, bias_part[None], (index // 2, 0))
    small = lax.psum(jnp.concatenate([partial_gain_grad, wide.reshape(-1)]), DP_FSDP)
    gain_grad = small[:d]
    bias_grad = lax.dynamic_slice(small[d:], (index * k,), (k,))
    scaled_values = normed_rows_gradient * norm_gain_vector
    final_result = packed_cot.astype(jnp.float32) + own_inverse * (
        scaled_values
        - jnp.mean(scaled_values, axis=1, keepdims=True)
        - local_standardized * jnp.mean(scaled_values * local_standardized, axis=1, keepdims=True)
    )
    return (final_result.astype(jnp.bfloat16), up_grad, bias_grad, down_grad, gain_grad)


def solution(mesh):
    finer = Mesh(
        mesh.devices.reshape(16, 2, 4, 2, 2), ("dp_0", "dp_1", "fsdp_0", "fsdp_1", "fsdp_2")
    )
    return jax.shard_map(
        shards,
        mesh=finer,
        in_specs=(
            P(DP_FSDP, None),
            P(DP_FSDP, None),
            P(DP_FSDP, None),
            P(),
            P(None, FSDP),
            P(FSDP),
            P(FSDP, None),
        ),
        out_specs=(P(DP_FSDP, None), P(None, FSDP), P(FSDP), P(FSDP, None), P()),
        check_vma=False,
    )
```

profile of v0, /device:TPU:2, one launch (start us, length us, event | category | flops | bytes accessed | tf_op | source)
XLA Modules:
  0.0 631.0 jit_solution(15258363506738329338)
XLA Ops:
  7.2 0.8 fusion.26
  8.1 0.8 select_reduce_fusion
  9.0 0.7 compare_select_fusion
  9.9 1.2 convolution_convert_fusion.3
  11.1 1.0 all_to_all.8
  12.1 16.6 %all-to-all-start = ((bf16[32,4,2048]{2,1,0:T(4,128)(2,1)}), bf16[32,4,2048]{2,1,0:T(4,128)(2,1)S(1)}, u32[]{:S(2)}, u32[]{:S(2)}) async-start(bf16[32,4,2048]{2,1,0:T(4,128)(2,1)} %all_to_all.8), calls=%async_computation | async-start | bytes 1048576 | tf_op jit(solution)/shard_map/all_to_all | solution.py:18
  28.8 1.0 copy.14
  29.9 31.9 %all-to-all-done = bf16[32,4,2048]{2,1,0:T(4,128)(2,1)S(1)} async-done(((bf16[32,4,2048]{2,1,0:T(4,128)(2,1)}), bf16[32,4,2048]{2,1,0:T(4,128)(2,1)S(1)}, u32[]{:S(2)}, u32[]{:S(2)}) %all-to-all-start) | async-done | bytes 524320 | tf_op jit(solution)/shard_map/all_to_all | solution.py:18
  62.2 0.9 fusion.18
  63.2 0.7 slice.24
  64.0 0.5 all-gather.9.cloned.1.call-update
  64.6 1.8 all-gather
  66.4 61.5 %all-gather.11.cloned.1.call-done = bf16[1024,1024]{1,0:T(8,128)(2,1)} async-done(((bf16[128,1024]{1,0:T(8,128)(2,1)}), bf16[1024,1024]{1,0:T(8,128)(2,1)}) %all-gather.11.cloned.1.call-update) | async-done | bytes 2097168 | tf_op jit(solution)/shard_map/all_gather | solution.py:69
  127.9 4.4 fusion.33
  132.4 68.8 %all-gather.7.cloned.1.call-done = bf16[1024,1024]{1,0:T(8,128)(2,1)} async-done(((bf16[128,1024]{1,0:T(8,128)(2,1)}), bf16[1024,1024]{1,0:T(8,128)(2,1)}) %all-gather.7.cloned.1.call-update) | async-done | bytes 2097168 | tf_op jit(solution)/shard_map/all_gather | solution.py:68
  201.1 3.6 convolution_convert_fusion.1
  204.8 17.0 %all-gather.9.cloned.1.call-done = bf16[512,1024]{1,0:T(8,128)(2,1)} async-done(((bf16[256,1024]{1,0:T(8,128)(2,1)}), bf16[512,1024]{1,0:T(8,128)(2,1)}) %all-gather.9.cloned.1.call-update) | async-done | bytes 1048592 | tf_op jit(solution)/shard_map/all_gather | solution.py:51
  221.8 5.1 convert_reduce_fusion
  226.9 1.3 fusion.7
  228.2 1.5 pad_maximum_fusion
  229.8 21.8 %reduce-scatter.6.cloned.1.call-done = bf16[256,2048]{1,0:T(8,128)(2,1)} async-done(((bf16[512,2048]{1,0:T(8,128)(2,1)}), bf16[256,2048]{1,0:T(8,128)(2,1)}) %reduce-scatter.6.cloned.1.call-update) | async-done | bytes 1048592 | tf_op jit(solution)/shard_map/reduce_scatter | solution.py:84
  251.6 2.6 convolution_convert_fusion
  254.3 139.2 %reduce-scatter.8.cloned.1.call-done = bf16[8,2048]{1,0:T(8,128)(2,1)} async-done(((bf16[256,2048]{1,0:T(8,128)(2,1)}), bf16[8,2048]{1,0:T(8,128)(2,1)}) %reduce-scatter.8.cloned.1.call-update) | async-done | bytes 32784 | tf_op jit(solution)/shard_map/reduce_scatter | solution.py:85
  393.7 100.6 %psum.7 = f32[5120]{0:T(1024)S(1)} all-reduce(f32[5120]{0:T(1024)S(1)} %pad_maximum_fusion.2), channel_id=1, replica_groups=mesh['dp_0'=16,'dp_1'=2,'fsdp_0'=4,'fsdp_1'=2,'fsdp_2'=2] {'dp_0','dp_1'..., use_global_device_ids=true, to_apply=%region_11.12 | all-reduce | flops 5120 | bytes 40960 | tf_op jit(solution)/shard_map/psum | solution.py:102
  494.2 0.6 slice.29
  494.8 0.6 dynamic_slice.3
  495.5 1.2 fusion.25
  496.7 1.9 fusion.23
  498.6 121.5 %all-gather.15.cloned.1.call-done = bf16[256,2048]{1,0:T(8,128)(2,1)} async-done(((bf16[8,2048]{1,0:T(8,128)(2,1)}), bf16[256,2048]{1,0:T(8,128)(2,1)}) %all-gather.15.cloned.1.call-update) | async-done | bytes 1048592 | tf_op jit(solution)/shard_map/all_gather | solution.py:86
  620.1 1.5 convert_element_type.58
  621.7 1.3 copy.15
  623.0 1.1 slice.28
  (51 shorter events, 1.6 us)
Async XLA Ops:
  7.2 2.5 copy-start
  9.6 19.1 %copy-start.2 = (bf16[1024,256]{1,0:T(8,128)(2,1)S(1)}, bf16[1024,256]{1,0:T(8,128)(2,1)}, u32[]{:S(2)}) copy-start(bf16[1024,256]{1,0:T(8,128)(2,1)} %param.11) | copy-start | bytes 1572868
  12.1 50.1 %copy-start.3 = (f32[1024]{0:T(1024)S(1)}, f32[1024]{0:T(1024)}, u32[]{:S(2)}) copy-start(f32[1024]{0:T(1024)} %param.10) | copy-start | bytes 12292
  12.1 49.7 %all-to-all-start = ((bf16[32,4,2048]{2,1,0:T(4,128)(2,1)}), bf16[32,4,2048]{2,1,0:T(4,128)(2,1)S(1)}, u32[]{:S(2)}, u32[]{:S(2)}) async-start(bf16[32,4,2048]{2,1,0:T(4,128)(2,1)} %all_to_all.8), calls=%async_computation | async-start | bytes 1048576 | tf_op jit(solution)/shard_map/all_to_all | solution.py:18
  28.7 37.7 %all-gather.13.cloned.1.call-start = ((), (), s32[]{:S(2)}) async-start(), calls=%async_computation.7 | async-start | bytes 1572864 | tf_op jit(solution)/shard_map/all_gather | solution.py:50
  29.8 34.8 %copy-start.4 = (f32[256]{0:T(256)S(1)}, f32[256]{0:T(256)}, u32[]{:S(2)}) copy-start(f32[256]{0:T(256)} %param.12) | copy-start | bytes 3076
  29.8 98.1 %all-gather.11.cloned.1.call-start = ((), (), s32[]{:S(2)}) async-start(), calls=%async_computation.6 | async-start | bytes 2359296 | tf_op jit(solution)/shard_map/all_gather | solution.py:69
  63.2 138.0 %all-gather.7.cloned.1.call-start = ((), (), s32[]{:S(2)}) async-start(), calls=%async_computation.4 | async-start | bytes 2359296 | tf_op jit(solution)/shard_map/all_gather | solution.py:68
  64.0 157.8 %all-gather.9.cloned.1.call-start = ((), (), s32[]{:S(2)}) async-start(), calls=%async_computation.5 | async-start | bytes 1572864 | tf_op jit(solution)/shard_map/all_gather | solution.py:51
  64.5 187.0 %reduce-scatter.6.cloned.1.call-start = ((), (), s32[]{:S(2)}) async-start(), calls=%async_computation.9 | async-start | bytes 3145728 | tf_op jit(solution)/shard_map/reduce_scatter | solution.py:84
  204.7 22.2 %copy-start.6 = (bf16[1024,512]{0,1:T(8,128)(2,1)S(1)}, bf16[1024,512]{0,1:T(8,128)(2,1)}, u32[]{:S(2)}) copy-start(bf16[1024,512]{0,1:T(8,128)(2,1)} %all-gather.13.cloned.1.call-done) | copy-start | bytes 3145732
  221.8 5.1 copy-start.5
  226.9 1.3 copy-start.7
  229.7 21.9 %copy-start.8 = (bf16[1024,512]{1,0:T(8,128)(2,1)S(1)}, bf16[1024,512]{1,0:T(8,128)(2,1)}, u32[]{:S(2)}) copy-start(bf16[1024,512]{1,0:T(8,128)(2,1)} %copy-done.7) | copy-start | bytes 3145732
  229.7 163.8 %reduce-scatter.8.cloned.1.call-start = ((), (), s32[]{:S(2)}) async-start(), calls=%async_computation.10 | async-start | bytes 1081344 | tf_op jit(solution)/shard_map/reduce_scatter | solution.py:85
  251.6 243.9 %reduce-scatter.4.cloned.1.call-start = ((), (), s32[]{:S(2)}) async-start(), calls=%async_computation.8 | async-start | bytes 2359296 | tf_op jit(solution)/shard_map/reduce_scatter | solution.py:90
  254.3 365.9 %all-gather.15.cloned.1.call-start = ((), (), s32[]{:S(2)}) async-start(), calls=%async_computation.11 | async-start | bytes 1081344 | tf_op jit(solution)/shard_map/all_gather | solution.py:86
  621.6 1.4 copy-start.1
Sparse Core Ops, SparseCore 0:
  32.2 20.3 all-gather.12
  63.3 64.5 all-gather.10
  131.7 69.3 all-gather.6
  203.1 18.6 all-gather.8
  229.9 21.6 reduce-scatter.5
  254.2 139.2 reduce-scatter.7
  398.2 89.2 reduce-scatter.3
  489.5 130.5 all-gather.14
where the time goes:
time: 631 us
  waiting for transfers between devices  462 us (73%)
  blocking collectives  102 us (16%)
  matrix products  18.4 us (3%)
  starting transfers between devices  17 us (3%)
  between operations  14.4 us (2%)
  other arithmetic  9.85 us (2%)
  local copies, waits for them, and re-layouts  6.69 us (1%)
    reduce_scatter x1, waiting for transfers between devices, shards(): mine = lax.psum_scatter(mine, DP, scatter_dimension=0, tiled=True)  139 us
    all_gather x1, waiting for transfers between devices, shards(): whole = lax.all_gather(mine, DP, axis=0, tiled=True).astype(jnp.float32)  122 us
    psum x1, blocking collectives, shards(): lax.psum(jnp.concatenate([partial_gain_grad, wide.reshape(-1)]), DP_FSDP)  101 us
    all_gather x1, waiting for transfers between devices, shards(): all_cot = lax.all_gather(packed_cot, ROWS_AXES, axis=0, tiled=True)  68.8 us
    all_gather x1, waiting for transfers between devices, shards(): lax.all_gather(normed_local, ROWS_AXES, axis=0, tiled=True)  61.5 us
    all_to_all x1, waiting for transfers between devices, side_by_side(): lax.all_to_all(both, axis, split_axis=split_dim, concat_axis=concat_dim,...  31.9 us
    reduce_scatter x1, waiting for transfers between devices, shards(): mine = lax.psum_scatter(parts, 'fsdp_2', scatter_dimension=0, tiled=True)  21.8 us
    all_gather x1, waiting for transfers between devices, shards(): down_weight = lax.all_gather(down_weight, 'fsdp_2', axis=0, tiled=True)  17 us
  transfers between devices with their start and end apart: 9, of which 7 were waited for; matrix products, arithmetic and copies ran while one was open for 3% of the time, Pallas kernels for 0%

commit v1 on v0

--- a/solution.py
+++ b/solution.py
@@ -83,7 +83,17 @@
     parts = jnp.concatenate([up_part, down_part], axis=1).astype(jnp.bfloat16)
     mine = lax.psum_scatter(parts, "fsdp_2", scatter_dimension=0, tiled=True)
     mine = lax.psum_scatter(mine, DP, scatter_dimension=0, tiled=True)
-    whole = lax.all_gather(mine, DP, axis=0, tiled=True).astype(jnp.float32)
+
+    def wall_compute(q_in, axis_id):
+        all_values = jnp.concatenate(
+            jax.lax.all_to_all(
+                jnp.stack([q_in for _ in range(jax.lax.psum(1, axis_id))]), axis_id, 0, 0
+            ),
+            axis=0,
+        )
+        return all_values
+
+    whole = wall_compute(mine, DP).astype(jnp.float32)
     d = up_weight.shape[0]
     up_grad = whole[:, :d].T
     down_grad = whole[:, d:]

time: 631 us -> 528 us (0.84)
  the two profiles are of different devices: /device:TPU:2 before, /device:TPU:1 now
where the time goes in v1:
time: 528 us
  waiting for transfers between devices  315 us (60%)
  blocking collectives  137 us (26%)
  starting transfers between devices  26.2 us (5%)
  matrix products  18.5 us (4%)
  between operations  14.4 us (3%)
  other arithmetic  8.66 us (2%)
  local copies, waits for them, and re-layouts  8.49 us (2%)
    psum x1, blocking collectives, shards(): lax.psum(jnp.concatenate([partial_gain_grad, wide.reshape(-1)]), DP_FSDP)  132 us
    reduce_scatter x1, waiting for transfers between devices, shards(): mine = lax.psum_scatter(mine, DP, scatter_dimension=0, tiled=True)  114 us
    all_gather x1, waiting for transfers between devices, shards(): all_cot = lax.all_gather(packed_cot, ROWS_AXES, axis=0, tiled=True)  68.8 us
    all_gather x1, waiting for transfers between devices, shards(): lax.all_gather(normed_local, ROWS_AXES, axis=0, tiled=True)  59.9 us
    all_to_all x1, waiting for transfers between devices, side_by_side(): lax.all_to_all(both, axis, split_axis=split_dim, concat_axis=concat_dim,...  30.2 us
    reduce_scatter x1, waiting for transfers between devices, shards(): mine = lax.psum_scatter(parts, 'fsdp_2', scatter_dimension=0, tiled=True)  21.2 us
    all_gather x1, waiting for transfers between devices, shards(): down_weight = lax.all_gather(down_weight, 'fsdp_2', axis=0, tiled=True)  19.7 us
    all_to_all x1, starting transfers between devices, side_by_side(): lax.all_to_all(both, axis, split_axis=split_dim, concat_axis=concat_dim,...  17.2 us
  transfers between devices with their start and end apart: 9, of which 6 were waited for; matrix products, arithmetic and copies ran while one was open for 4% of the time, Pallas kernels for 0%

profile of v1, /device:TPU:1, one launch (start us, length us, event | category | flops | bytes accessed | tf_op | source)
XLA Modules:
  0.0 527.6 jit_solution(5952640362095758041)
XLA Ops:
  7.2 0.8 fusion.26
  8.1 0.8 select_reduce_fusion
  9.0 0.7 compare_select_fusion
  9.9 1.2 convolution_convert_fusion.3
  11.1 1.0 all_to_all.11
  12.1 17.2 %all-to-all-start = ((bf16[32,4,2048]{2,1,0:T(4,128)(2,1)}), bf16[32,4,2048]{2,1,0:T(4,128)(2,1)S(1)}, u32[]{:S(2)}, u32[]{:S(2)}) async-start(bf16[32,4,2048]{2,1,0:T(4,128)(2,1)} %all_to_all.11), calls=%async_computation | async-start | bytes 1048576 | tf_op jit(solution)/shard_map/all_to_all | solution.py:18
  29.3 1.0 copy.14
  30.4 30.2 %all-to-all-done = bf16[32,4,2048]{2,1,0:T(4,128)(2,1)S(1)} async-done(((bf16[32,4,2048]{2,1,0:T(4,128)(2,1)}), bf16[32,4,2048]{2,1,0:T(4,128)(2,1)S(1)}, u32[]{:S(2)}, u32[]{:S(2)}) %all-to-all-start) | async-done | bytes 524320 | tf_op jit(solution)/shard_map/all_to_all | solution.py:18
  61.1 0.9 fusion.18
  62.1 0.7 slice.24
  62.9 0.5 all-gather.8.cloned.1.call-update
  63.5 4.1 all-gather
  67.6 59.9 %all-gather.10.cloned.1.call-done = bf16[1024,1024]{1,0:T(8,128)(2,1)} async-done(((bf16[128,1024]{1,0:T(8,128)(2,1)}), bf16[1024,1024]{1,0:T(8,128)(2,1)}) %all-gather.10.cloned.1.call-update) | async-done | bytes 2097168 | tf_op jit(solution)/shard_map/all_gather | solution.py:69
  127.5 4.5 fusion.34
  132.0 68.8 %all-gather.6.cloned.1.call-done = bf16[1024,1024]{1,0:T(8,128)(2,1)} async-done(((bf16[128,1024]{1,0:T(8,128)(2,1)}), bf16[1024,1024]{1,0:T(8,128)(2,1)}) %all-gather.6.cloned.1.call-update) | async-done | bytes 2097168 | tf_op jit(solution)/shard_map/all_gather | solution.py:68
  200.7 3.6 convolution_convert_fusion.1
  204.3 19.7 %all-gather.8.cloned.1.call-done = bf16[512,1024]{1,0:T(8,128)(2,1)} async-done(((bf16[256,1024]{1,0:T(8,128)(2,1)}), bf16[512,1024]{1,0:T(8,128)(2,1)}) %all-gather.8.cloned.1.call-update) | async-done | bytes 1048592 | tf_op jit(solution)/shard_map/all_gather | solution.py:51
  224.1 5.1 convert_reduce_fusion
  229.2 1.3 fusion.7
  230.5 1.5 pad_maximum_fusion
  232.1 21.2 %reduce-scatter.6.cloned.1.call-done = bf16[256,2048]{1,0:T(8,128)(2,1)} async-done(((bf16[512,2048]{1,0:T(8,128)(2,1)}), bf16[256,2048]{1,0:T(8,128)(2,1)}) %reduce-scatter.6.cloned.1.call-update) | async-done | bytes 1048592 | tf_op jit(solution)/shard_map/reduce_scatter | solution.py:84
  253.4 2.6 convolution_convert_fusion
  256.0 114.5 %reduce-scatter.8.cloned.1.call-done = bf16[8,2048]{1,0:T(8,128)(2,1)} async-done(((bf16[256,2048]{1,0:T(8,128)(2,1)}), bf16[8,2048]{1,0:T(8,128)(2,1)}) %reduce-scatter.8.cloned.1.call-update) | async-done | bytes 32784 | tf_op jit(solution)/shard_map/reduce_scatter | solution.py:85
  370.5 1.8 stack.2
  372.4 8.7 %all-to-all-start.1 = ((bf16[32,8,2048]{2,1,0:T(8,128)(2,1)}), bf16[32,8,2048]{2,1,0:T(8,128)(2,1)S(1)}, u32[]{:S(2)}, u32[]{:S(2)}) async-start(bf16[32,8,2048]{2,1,0:T(8,128)(2,1)} %stack.2), calls=%async_computation.4 | async-start | bytes 2097152 | tf_op jit(solution)/shard_map/all_to_all | solution.py:89
  381.2 132.4 %psum.7 = f32[5120]{0:T(1024)S(1)} all-reduce(f32[5120]{0:T(1024)S(1)} %pad_maximum_fusion.2), channel_id=1, replica_groups=mesh['dp_0'=16,'dp_1'=2,'fsdp_0'=4,'fsdp_1'=2,'fsdp_2'=2] {'dp_0','dp_1'..., use_global_device_ids=true, to_apply=%region_11.12 | all-reduce | flops 5120 | bytes 40960 | tf_op jit(solution)/shard_map/psum | solution.py:112
  513.7 0.6 slice.29
  514.3 0.6 dynamic_slice.3
  514.9 1.2 fusion.25
  516.1 1.9 fusion.23
  518.3 1.2 fusion.33
  519.4 1.3 copy.15
  (48 shorter events, 1.6 us)
Async XLA Ops:
  7.2 2.5 copy-start
  9.6 19.7 %copy-start.1 = (bf16[1024,256]{1,0:T(8,128)(2,1)S(1)}, bf16[1024,256]{1,0:T(8,128)(2,1)}, u32[]{:S(2)}) copy-start(bf16[1024,256]{1,0:T(8,128)(2,1)} %param.11) | copy-start | bytes 1572868
  12.1 49.0 %copy-start.2 = (f32[1024]{0:T(1024)S(1)}, f32[1024]{0:T(1024)}, u32[]{:S(2)}) copy-start(f32[1024]{0:T(1024)} %param.10) | copy-start | bytes 12292
  12.1 48.5 %all-to-all-start = ((bf16[32,4,2048]{2,1,0:T(4,128)(2,1)}), bf16[32,4,2048]{2,1,0:T(4,128)(2,1)S(1)}, u32[]{:S(2)}, u32[]{:S(2)}) async-start(bf16[32,4,2048]{2,1,0:T(4,128)(2,1)} %all_to_all.11), calls=%async_computation | async-start | bytes 1048576 | tf_op jit(solution)/shard_map/all_to_all | solution.py:18
  29.2 38.3 %all-gather.12.cloned.1.call-start = ((), (), s32[]{:S(2)}) async-start(), calls=%async_computation.8 | async-start | bytes 1572864 | tf_op jit(solution)/shard_map/all_gather | solution.py:50
  30.3 33.1 %copy-start.3 = (f32[256]{0:T(256)S(1)}, f32[256]{0:T(256)}, u32[]{:S(2)}) copy-start(f32[256]{0:T(256)} %param.12) | copy-start | bytes 3076
  30.3 97.2 %all-gather.10.cloned.1.call-start = ((), (), s32[]{:S(2)}) async-start(), calls=%async_computation.7 | async-start | bytes 2359296 | tf_op jit(solution)/shard_map/all_gather | solution.py:69
  62.0 138.7 %all-gather.6.cloned.1.call-start = ((), (), s32[]{:S(2)}) async-start(), calls=%async_computation.5 | async-start | bytes 2359296 | tf_op jit(solution)/shard_map/all_gather | solution.py:68
  62.8 161.2 %all-gather.8.cloned.1.call-start = ((), (), s32[]{:S(2)}) async-start(), calls=%async_computation.6 | async-start | bytes 1572864 | tf_op jit(solution)/shard_map/all_gather | solution.py:51
  63.4 189.9 %reduce-scatter.6.cloned.1.call-start = ((), (), s32[]{:S(2)}) async-start(), calls=%async_computation.10 | async-start | bytes 3145728 | tf_op jit(solution)/shard_map/reduce_scatter | solution.py:84
  204.3 24.9 %copy-start.5 = (bf16[1024,512]{0,1:T(8,128)(2,1)S(1)}, bf16[1024,512]{0,1:T(8,128)(2,1)}, u32[]{:S(2)}) copy-start(bf16[1024,512]{0,1:T(8,128)(2,1)} %all-gather.12.cloned.1.call-done) | copy-start | bytes 3145732
  224.1 5.1 copy-start.4
  229.2 1.3 copy-start.6
  232.0 21.4 %copy-start.7 = (bf16[1024,512]{1,0:T(8,128)(2,1)S(1)}, bf16[1024,512]{1,0:T(8,128)(2,1)}, u32[]{:S(2)}) copy-start(bf16[1024,512]{1,0:T(8,128)(2,1)} %copy-done.6) | copy-start | bytes 3145732
  232.1 138.4 %reduce-scatter.8.cloned.1.call-start = ((), (), s32[]{:S(2)}) async-start(), calls=%async_computation.11 | async-start | bytes 1081344 | tf_op jit(solution)/shard_map/reduce_scatter | solution.py:85
  253.4 261.5 %reduce-scatter.4.cloned.1.call-start = ((), (), s32[]{:S(2)}) async-start(), calls=%async_computation.9 | async-start | bytes 2359296 | tf_op jit(solution)/shard_map/reduce_scatter | solution.py:100
  372.4 145.7 %all-to-all-start.1 = ((bf16[32,8,2048]{2,1,0:T(8,128)(2,1)}), bf16[32,8,2048]{2,1,0:T(8,128)(2,1)S(1)}, u32[]{:S(2)}, u32[]{:S(2)}) async-start(bf16[32,8,2048]{2,1,0:T(8,128)(2,1)} %stack.2), calls=%async_computation.4 | async-start | bytes 2097152 | tf_op jit(solution)/shard_map/all_to_all | solution.py:89
Sparse Core Ops, SparseCore 0:
  32.7 22.0 all-gather.11
  62.2 65.2 all-gather.9
  131.3 69.3 all-gather.5
  202.7 21.3 all-gather.7
  232.2 21.0 reduce-scatter.5
  256.0 114.4 reduce-scatter.7
  375.1 115.9 reduce-scatter.3
